TPU v7x, 32 devices: a whole 2x2x4 slice. The times are simulated.
32 devices in a mesh: row: 4 (over y, x), col: 4 (over z), depth: 2 (over core).
Axes of the slice: x: 2, y: 2, z: 4, core: 2. Of those that a mesh axis runs over, the one named last changes fastest.
Arguments:
- matrix_panel: bfloat16 [12288, 65536], P('row', 'col'), may hold values from -0.1484375 to 0.1484375
- start_block: bfloat16 [12288, 64], P('row', 'depth'), may hold values from -6 to 6
- stored_basis: float32 [12288, 1024], P('row'), may hold values from -2.2 to 2.2
Outputs:
- new_block: float32 [12288, 64], P('row', 'depth')
- coefficients: float32 [1024, 64], P(None, 'depth')
- triangle: float32 [64, 64], replicated
All inputs are finite; a program needn't handle non-finite values.
Results may differ from a plain program's by a relative error of at most 0.0023.
Values may be sent and summed in bfloat16 or wider, within the bound.
A program may use at most 256 MiB of HBM per device.

v0:
```python
import jax
import jax.numpy as jnp
from jax import lax
from jax.sharding import PartitionSpec as P

HIGHEST = lax.Precision.HIGHEST


def contract_rows(left_side, right_side, mode):
    return lax.dot_general(
        left_side,
        right_side,
        (((0,), (0,)), ((), ())),
        precision=mode,
        preferred_element_type=jnp.float32,
    )


def factor_gram(gram_matrix):
    lower_factor = jnp.linalg.cholesky(gram_matrix)
    identity = jnp.eye(gram_matrix.shape[0], dtype=jnp.float32)
    inverse = jax.scipy.linalg.solve_triangular(lower_factor, identity, lower=True)
    return (lower_factor, inverse)


def orthonormal_pass(stored_basis, block_cols, reduce_sum, row_total):
    projection = reduce_sum(contract_rows(stored_basis, block_cols, HIGHEST)) / row_total
    remainder = block_cols - jnp.dot(
        stored_basis, projection, precision=HIGHEST, preferred_element_type=jnp.float32
    )
    gram_matrix = reduce_sum(contract_rows(remainder, remainder, HIGHEST)) / row_total
    lower_factor, inverse = factor_gram(gram_matrix)
    normed = jnp.dot(remainder, inverse.T, precision=HIGHEST, preferred_element_type=jnp.float32)
    return (projection, lower_factor, normed)


def per_device(matrix_panel, start_block, stored_basis):
    row_total = stored_basis.shape[0] * lax.axis_size("row")
    half_cols = start_block.shape[1]
    depth_index = lax.axis_index("depth")
    whole_start = lax.all_gather(start_block, "depth", axis=1, tiled=True)
    half_rows = matrix_panel.shape[0] // 2
    panel_rows = lax.dynamic_slice_in_dim(matrix_panel, depth_index * half_rows, half_rows, 0)
    start_rows = lax.dynamic_slice_in_dim(whole_start, depth_index * half_rows, half_rows, 0)
    basis_rows = lax.dynamic_slice_in_dim(stored_basis, depth_index * half_rows, half_rows, 0)
    mixed_cols = lax.psum(contract_rows(panel_rows, start_rows, None), ("row", "depth")).astype(
        jnp.bfloat16
    )
    image_block = lax.psum(
        jnp.dot(panel_rows, mixed_cols, preferred_element_type=jnp.float32), "col"
    )

    def sum_layers(value):
        return lax.psum(value, ("row", "depth"))

    proj_first, lower_first, normed_first = orthonormal_pass(
        basis_rows, image_block, sum_layers, row_total
    )
    proj_second, lower_second, normed_second = orthonormal_pass(
        basis_rows, normed_first, sum_layers, row_total
    )
    new_block = lax.all_to_all(normed_second, "depth", split_axis=1, concat_axis=0, tiled=True)
    coef_whole = proj_first + jnp.dot(
        proj_second, lower_first.T, precision=HIGHEST, preferred_element_type=jnp.float32
    )
    coefficients = lax.dynamic_slice_in_dim(coef_whole, depth_index * half_cols, half_cols, 1)
    triangle = jnp.dot(
        lower_second.T, lower_first.T, precision=HIGHEST, preferred_element_type=jnp.float32
    )
    return (new_block, coefficients, triangle)


def solution(mesh):
    placed = (P("row", "col"), P("row", "depth"), P("row", None))
    return jax.shard_map(
        per_device,
        mesh=mesh,
        in_specs=placed,
        out_specs=(P("row", "depth"), P(None, "depth"), P()),
        check_vma=False,
    )
```

profile of v0, /device:TPU:0, one launch (start us, length us, event | category | flops | bytes accessed | tf_op | source)
XLA Modules:
  0.0 405.6 jit_solution(3928022254567349980)
XLA Ops:
  7.2 2.4 all_gather.3
  9.6 20.5 %fusion.2 = f32[16384,64]{0,1:T(8,128)} fusion(bf16[3072,16384]{1,0:T(8,128)(2,1)} %param.6, s32[]{:T(128)S(6)} %select_n.11, bf16[3072,64]{0,1:T(8,128)(2,1)S(1)} %all_gather.3), kind=kOutput, calls=%fused_computation.2 | convolution fusion | flops 3221225472 | bytes 54723584 | tf_op jit(solution)/shard_map/dot_general | solution.py:10
  30.1 89.5 %all-reduce.10 = bf16[16384,64]{0,1:T(8,128)(2,1)S(1)} all-reduce(f32[16384,64]{0,1:T(8,128)} %fusion.2), channel_id=1, replica_groups=mesh['row'=4,'col'=4,'depth'=2] {'row','depth'}, use_global_device_ids=true, to_apply=%region_0.0 | all-reduce | flops 1048576 | bytes 6291456 | tf_op jit(solution)/shard_map/psum | solution.py:46
  119.6 22.6 %fusion = f32[1536,64]{0,1:T(8,128)} fusion(bf16[3072,16384]{1,0:T(8,128)(2,1)} %param.6, s32[]{:T(128)S(6)} %select_n.11, bf16[16384,64]{0,1:T(8,128)(2,1)S(1)} %all-reduce.10), kind=kOutput, calls=%fused_computation | convolution fusion | flops 3221225472 | bytes 52822020 | tf_op jit(solution)/shard_map/dot_general | solution.py:50
  142.3 36.9 %all-reduce.5.cloned.1.call-done = f32[1536,64]{0,1:T(8,128)} async-done(((f32[1536,64]{0,1:T(8,128)}), f32[1536,64]{0,1:T(8,128)}) %all-reduce.5.cloned.1.call-update) | async-done | bytes 393232 | tf_op jit(solution)/shard_map/psum | solution.py:49
  179.2 7.6 %fusion.10 = f32[1024,64]{0,1:T(8,128)} fusion(f32[1536,64]{0,1:T(8,128)} %all-reduce.5.cloned.1.call-done, f32[3072,1024]{1,0:T(8,128)} %param.8, s32[]{:T(128)S(6)} %select_n.11), kind=kOutput, calls=%fused_computation.10 | convolution fusion | flops 1207959552 | bytes 6946820 | tf_op jit(solution)/shard_map/dot_general | solution.py:10
  187.0 53.1 %all-reduce.7.cloned.1.call-done = f32[1024,64]{0,1:T(8,128)} async-done(((f32[1024,64]{0,1:T(8,128)}), f32[1024,64]{0,1:T(8,128)}) %all-reduce.7.cloned.1.call-update) | async-done | bytes 262160 | tf_op jit(solution)/shard_map/psum | solution.py:54
  240.1 9.1 %fusion.12 = f32[1536,64]{0,1:T(8,128)S(1)} fusion(f32[1536,64]{0,1:T(8,128)} %all-reduce.5.cloned.1.call-done, f32[3072,1024]{1,0:T(8,128)} %param.8, s32[]{:T(128)S(6)} %select_n.11, f32[1024,64]{0,1:T(8,128)} %all-reduce.7.cloned.1.call-done), kind=kOutput, calls=%fused_computation.12 | convolution fusion | flops 1208123392 | bytes 7340036 | tf_op jit(solution)/shard_map/dot_general | solution.py:28
  249.2 0.5 fusion.56
  249.6 22.4 %psum.45 = f32[64,64]{0,1:T(8,128)S(1)} all-reduce(f32[64,64]{0,1:T(8,128)S(1)} %fusion.56), channel_id=1, replica_groups=mesh['row'=4,'col'=4,'depth'=2] {'row','depth'}, use_global_device_ids=true, to_apply=%region_3.0 | all-reduce | flops 4096 | bytes 32768 | tf_op jit(solution)/shard_map/psum | solution.py:54
  272.1 5.8 %cholesky.44 = f32[64,64]{1,0:T(8,128)S(1)} custom-call(f32[64,64]{1,0:T(8,128)S(1)} %fusion.32), custom_call_target="Cholesky" | custom-call | tf_op jit(solution)/shard_map/jit(cholesky)/cholesky | solution.py:20
  278.0 0.6 compare_reduce_fusion.1
  278.6 0.7 select_bitcast_fusion.1
  279.3 4.9 %custom-call.6 = f32[1,64,64]{1,2,0:T(8,128)S(1)} custom-call(f32[1,64,64]{2,1,0:T(8,128)S(1)} %select_bitcast_fusion.1), custom_call_target="InvertDiagBlocksLowerTriangular" | custom-call | tf_op jit(solution)/shard_map/jit(_solve_triangular)/triangular_solve | solution.py:22
  284.2 0.3 fusion.27
  284.4 0.5 fusion.57
  284.9 7.6 %fusion.6 = f32[1024,64]{0,1:T(8,128)} fusion(f32[1536,64]{0,1:T(8,128)S(1)} %fusion.57, f32[3072,1024]{1,0:T(8,128)} %param.8, s32[]{:T(128)S(6)} %select_n.11), kind=kOutput, calls=%fused_computation.6 | convolution fusion | flops 1207959552 | bytes 6946820 | tf_op jit(solution)/shard_map/dot_general | solution.py:10
  292.5 53.0 %all-reduce.9.cloned.1.call-done = f32[1024,64]{0,1:T(8,128)} async-done(((f32[1024,64]{0,1:T(8,128)}), f32[1024,64]{0,1:T(8,128)}) %all-reduce.9.cloned.1.call-update) | async-done | bytes 262160 | tf_op jit(solution)/shard_map/psum | solution.py:54
  345.5 8.1 %fusion.15 = f32[1536,64]{0,1:T(8,128)S(1)} fusion(f32[1536,64]{0,1:T(8,128)S(1)} %fusion.57, f32[3072,1024]{1,0:T(8,128)} %param.8, s32[]{:T(128)S(6)} %select_n.11, f32[1024,64]{0,1:T(8,128)} %all-reduce.9.cloned.1.call-done), kind=kOutput, calls=%fused_computation.13 | convolution fusion | flops 1208123392 | bytes 7340036 | tf_op jit(solution)/shard_map/dot_general | solution.py:28
  353.7 0.5 fusion.58
  354.1 22.4 %psum.47 = f32[64,64]{0,1:T(8,128)S(1)} all-reduce(f32[64,64]{0,1:T(8,128)S(1)} %fusion.58), channel_id=1, replica_groups=mesh['row'=4,'col'=4,'depth'=2] {'row','depth'}, use_global_device_ids=true, to_apply=%region_7.10 | all-reduce | flops 4096 | bytes 32768 | tf_op jit(solution)/shard_map/psum | solution.py:54
  376.6 5.8 %cholesky.55 = f32[64,64]{1,0:T(8,128)S(1)} custom-call(f32[64,64]{1,0:T(8,128)S(1)} %fusion.30), custom_call_target="Cholesky" | custom-call | tf_op jit(solution)/shard_map/jit(cholesky)/cholesky | solution.py:20
  382.5 0.6 compare_reduce_fusion
  383.1 2.1 fusion.34
  385.3 0.7 select_bitcast_fusion
  385.9 4.9 %custom-call.7 = f32[1,64,64]{1,2,0:T(8,128)S(1)} custom-call(f32[1,64,64]{2,1,0:T(8,128)S(1)} %select_bitcast_fusion), custom_call_target="InvertDiagBlocksLowerTriangular" | custom-call | tf_op jit(solution)/shard_map/jit(_solve_triangular)/triangular_solve | solution.py:22
  390.8 0.3 fusion.25
  391.1 0.5 fusion.59
  391.6 4.0 all_to_all.19
  395.6 0.8 copy.18
  396.4 2.0 fusion.19
  398.4 0.7 dynamic-slice_add_fusion
  (17 shorter events, 0.6 us)
Async XLA Ops:
  7.2 172.0 %all-reduce.5.cloned.1.call-start = ((), (), s32[]{:S(2)}) async-start(), calls=%async_computation.1 | async-start | bytes 786432 | tf_op jit(solution)/shard_map/psum | solution.py:49
  142.2 97.8 %all-reduce.7.cloned.1.call-start = ((), (), s32[]{:S(2)}) async-start(), calls=%async_computation.2 | async-start | bytes 524288 | tf_op jit(solution)/shard_map/psum | solution.py:54
  186.8 158.8 %all-reduce.9.cloned.1.call-start = ((), (), s32[]{:S(2)}) async-start(), calls=%async_computation.3 | async-start | bytes 524288 | tf_op jit(solution)/shard_map/psum | solution.py:54
  240.1 52.4 %copy-start = (f32[1024,64]{0,1:T(8,128)S(1)}, f32[1024,64]{0,1:T(8,128)}, u32[]{:S(2)}) copy-start(f32[1024,64]{0,1:T(8,128)} %all-reduce.7.cloned.1.call-done) | copy-start | bytes 786436
Sparse Core Ops, SparseCore 0:
  142.3 36.8 all-reduce.4
  186.9 53.1 all-reduce.6
  292.6 52.8 all-reduce.8
where the time goes:
time: 406 us
  waiting for transfers between devices  143 us (35%)
  blocking collectives  141 us (35%)
  matrix products  82 us (20%)
  other arithmetic  24.9 us (6%)
  between operations  13.9 us (3%)
    psum x2, waiting for transfers between devices, sum_layers(): return lax.psum(value, ('row', 'depth'))  106 us
    psum x1, blocking collectives, per_device(): lax.psum(contract_rows(panel_rows, start_rows, None), ('row', 'depth'))  89.5 us
    psum x2, blocking collectives, sum_layers(): return lax.psum(value, ('row', 'depth'))  44.7 us
    psum x1, waiting for transfers between devices, per_device(): lax.psum(jnp.dot(panel_rows, mixed_cols, preferred_element_type=jnp.float...  36.9 us
    dot_general x5, matrix products, contract_rows(): lax.dot_general(left_side, right_side, (((0,), (0,)), ((), ())), precisio...  36.5 us
    dot_general x1, matrix products, per_device(): jnp.dot(panel_rows, mixed_cols, preferred_element_type=jnp.float32)  22.6 us
    dot_general x2, matrix products, orthonormal_pass(): jnp.dot(stored_basis, projection, precision=HIGHEST, preferred_element_ty...  17.2 us
    another operation x6, other arithmetic, factor_gram(): lower_factor = jnp.linalg.cholesky(gram_matrix)  13 us
  transfers between devices with their start and end apart: 3, of which 3 were waited for; matrix products, arithmetic and copies ran while one was open for 0% of the time, Pallas kernels for 0%

commit v1 on v0

--- a/solution.py
+++ b/solution.py
@@ -51,7 +51,7 @@
     )
 
     def sum_layers(value):
-        return lax.psum(value, ("row", "depth"))
+        return lax.psum(lax.psum(value, "depth"), "row")
 
     proj_first, lower_first, normed_first = orthonormal_pass(
         basis_rows, image_block, sum_layers, row_total

time: 406 us -> 423 us (1.042)
  waiting for transfers between devices: 143 us -> 167 us
  blocking collectives: 141 us -> 133 us
    psum x2 -> x4, waiting for transfers between devices: 106 us -> 130 us  [sum_layers(): return lax.psum(lax.psum(value, 'depth'), 'row')]
    psum x2 -> x4, blocking collectives: 44.7 us -> 37.5 us  [sum_layers(): return lax.psum(lax.psum(value, 'depth'), 'row')]
  transfers between devices with their start and end apart: 3 -> 5, of which waited for: 3 -> 5; matrix products, arithmetic and copies ran while one was open for 0% -> 0% of each run, Pallas kernels for 0% -> 0%
where the time goes in v1:
time: 423 us; the launch traced here: 422 us
  waiting for transfers between devices  167 us (39%)
  blocking collectives  133 us (31%)
  matrix products  82 us (19%)
  other arithmetic  24.9 us (6%)
  between operations  13.9 us (3%)
    psum x4, waiting for transfers between devices, sum_layers(): return lax.psum(lax.psum(value, 'depth'), 'row')  130 us
    psum x1, blocking collectives, per_device(): lax.psum(contract_rows(panel_rows, start_rows, None), ('row', 'depth'))  89.5 us
    psum x4, blocking collectives, sum_layers(): return lax.psum(lax.psum(value, 'depth'), 'row')  37.5 us
    psum x1, waiting for transfers between devices, per_device(): lax.psum(jnp.dot(panel_rows, mixed_cols, preferred_element_type=jnp.float...  36.9 us
    dot_general x5, matrix products, contract_rows(): lax.dot_general(left_side, right_side, (((0,), (0,)), ((), ())), precisio...  36.5 us
    dot_general x1, matrix products, per_device(): jnp.dot(panel_rows, mixed_cols, preferred_element_type=jnp.float32)  22.6 us
    dot_general x2, matrix products, orthonormal_pass(): jnp.dot(stored_basis, projection, precision=HIGHEST, preferred_element_ty...  17.2 us
    another operation x6, other arithmetic, factor_gram(): lower_factor = jnp.linalg.cholesky(gram_matrix)  13 us
  transfers between devices with their start and end apart: 5, of which 5 were waited for; matrix products, arithmetic and copies ran while one was open for 0% of the time, Pallas kernels for 0%

profile of v1, /device:TPU:0, one launch (start us, length us, event | category | flops | bytes accessed | tf_op | source)
XLA Modules:
  0.0 422.5 jit_solution(11012168473042099243)
XLA Ops:
  7.2 2.4 all_gather.3
  9.6 20.5 %fusion.2 = f32[16384,64]{0,1:T(8,128)} fusion(bf16[3072,16384]{1,0:T(8,128)(2,1)} %param.6, s32[]{:T(128)S(6)} %select_n.11, bf16[3072,64]{0,1:T(8,128)(2,1)S(1)} %all_gather.3), kind=kOutput, calls=%fused_computation.2 | convolution fusion | flops 3221225472 | bytes 54723584 | tf_op jit(solution)/shard_map/dot_general | solution.py:10
  30.1 89.5 %all-reduce.16 = bf16[16384,64]{0,1:T(8,128)(2,1)S(1)} all-reduce(f32[16384,64]{0,1:T(8,128)} %fusion.2), channel_id=1, replica_groups=mesh['row'=4,'col'=4,'depth'=2] {'row','depth'}, use_global_device_ids=true, to_apply=%region_0.0 | all-reduce | flops 1048576 | bytes 6291456 | tf_op jit(solution)/shard_map/psum | solution.py:46
  119.6 22.6 %fusion = f32[1536,64]{0,1:T(8,128)} fusion(bf16[3072,16384]{1,0:T(8,128)(2,1)} %param.6, s32[]{:T(128)S(6)} %select_n.11, bf16[16384,64]{0,1:T(8,128)(2,1)S(1)} %all-reduce.16), kind=kOutput, calls=%fused_computation | convolution fusion | flops 3221225472 | bytes 52822020 | tf_op jit(solution)/shard_map/dot_general | solution.py:50
  142.3 36.9 %all-reduce.7.cloned.1.call-done = f32[1536,64]{0,1:T(8,128)} async-done(((f32[1536,64]{0,1:T(8,128)}), f32[1536,64]{0,1:T(8,128)}) %all-reduce.7.cloned.1.call-update) | async-done | bytes 393232 | tf_op jit(solution)/shard_map/psum | solution.py:49
  179.2 7.6 %fusion.10 = f32[1024,64]{0,1:T(8,128)} fusion(f32[1536,64]{0,1:T(8,128)} %all-reduce.7.cloned.1.call-done, f32[3072,1024]{1,0:T(8,128)} %param.8, s32[]{:T(128)S(6)} %select_n.11), kind=kOutput, calls=%fused_computation.10 | convolution fusion | flops 1207959552 | bytes 6946820 | tf_op jit(solution)/shard_map/dot_general | solution.py:10
  186.8 18.0 %all-reduce.9.cloned.1.call-done = f32[1024,64]{0,1:T(8,128)} async-done(((f32[1024,64]{0,1:T(8,128)}), f32[1024,64]{0,1:T(8,128)}) %all-reduce.9.cloned.1.call-update) | async-done | bytes 262160 | tf_op jit(solution)/shard_map/psum | solution.py:54
  205.1 46.8 %all-reduce.11.cloned.1.call-done = f32[1024,64]{0,1:T(8,128)} async-done(((f32[1024,64]{0,1:T(8,128)}), f32[1024,64]{0,1:T(8,128)}) %all-reduce.11.cloned.1.call-update) | async-done | bytes 262160 | tf_op jit(solution)/shard_map/psum | solution.py:54
  251.9 9.1 %fusion.12 = f32[1536,64]{0,1:T(8,128)S(1)} fusion(f32[1536,64]{0,1:T(8,128)} %all-reduce.7.cloned.1.call-done, f32[3072,1024]{1,0:T(8,128)} %param.8, s32[]{:T(128)S(6)} %select_n.11, f32[1024,64]{0,1:T(8,128)} %all-reduce.11.cloned.1.call-done), kind=kOutput, calls=%fused_computation.12 | convolution fusion | flops 1208123392 | bytes 7340036 | tf_op jit(solution)/shard_map/dot_general | solution.py:28
  261.4 3.4 psum.74
  264.9 15.3 %psum.75 = f32[64,64]{0,1:T(8,128)S(1)} all-reduce(f32[64,64]{0,1:T(8,128)S(1)} %psum.74), channel_id=1, replica_groups=mesh['row'=4,'col'=4,'depth'=2] {'row'}, use_global_device_ids=true, to_apply=%region_5.0 | all-reduce | flops 4096 | bytes 32768 | tf_op jit(solution)/shard_map/psum | solution.py:54
  280.3 5.8 %cholesky.44 = f32[64,64]{1,0:T(8,128)S(1)} custom-call(f32[64,64]{1,0:T(8,128)S(1)} %fusion.32), custom_call_target="Cholesky" | custom-call | tf_op jit(solution)/shard_map/jit(cholesky)/cholesky | solution.py:20
  286.2 0.6 compare_reduce_fusion.1
  286.8 0.7 select_bitcast_fusion.1
  287.5 4.9 %custom-call.6 = f32[1,64,64]{1,2,0:T(8,128)S(1)} custom-call(f32[1,64,64]{2,1,0:T(8,128)S(1)} %select_bitcast_fusion.1), custom_call_target="InvertDiagBlocksLowerTriangular" | custom-call | tf_op jit(solution)/shard_map/jit(_solve_triangular)/triangular_solve | solution.py:22
  292.7 0.5 fusion.57
  293.2 7.6 %fusion.6 = f32[1024,64]{0,1:T(8,128)} fusion(f32[1536,64]{0,1:T(8,128)S(1)} %fusion.57, f32[3072,1024]{1,0:T(8,128)} %param.8, s32[]{:T(128)S(6)} %select_n.11), kind=kOutput, calls=%fused_computation.6 | convolution fusion | flops 1207959552 | bytes 6946820 | tf_op jit(solution)/shard_map/dot_general | solution.py:10
  301.0 18.1 %all-reduce.13.cloned.1.call-done = f32[1024,64]{0,1:T(8,128)} async-done(((f32[1024,64]{0,1:T(8,128)}), f32[1024,64]{0,1:T(8,128)}) %all-reduce.13.cloned.1.call-update) | async-done | bytes 262160 | tf_op jit(solution)/shard_map/psum | solution.py:54
  319.2 46.8 %all-reduce.15.cloned.1.call-done = f32[1024,64]{0,1:T(8,128)} async-done(((f32[1024,64]{0,1:T(8,128)}), f32[1024,64]{0,1:T(8,128)}) %all-reduce.15.cloned.1.call-update) | async-done | bytes 262160 | tf_op jit(solution)/shard_map/psum | solution.py:54
  366.0 8.1 %fusion.15 = f32[1536,64]{0,1:T(8,128)S(1)} fusion(f32[1536,64]{0,1:T(8,128)S(1)} %fusion.57, f32[3072,1024]{1,0:T(8,128)} %param.8, s32[]{:T(128)S(6)} %select_n.11, f32[1024,64]{0,1:T(8,128)} %all-reduce.15.cloned.1.call-done), kind=kOutput, calls=%fused_computation.13 | convolution fusion | flops 1208123392 | bytes 7340036 | tf_op jit(solution)/shard_map/dot_general | solution.py:28
  374.6 3.4 psum.78
  378.0 15.4 %psum.79 = f32[64,64]{0,1:T(8,128)S(1)} all-reduce(f32[64,64]{0,1:T(8,128)S(1)} %psum.78), channel_id=1, replica_groups=mesh['row'=4,'col'=4,'depth'=2] {'row'}, use_global_device_ids=true, to_apply=%region_11.14 | all-reduce | flops 4096 | bytes 32768 | tf_op jit(solution)/shard_map/psum | solution.py:54
  393.5 5.8 %cholesky.55 = f32[64,64]{1,0:T(8,128)S(1)} custom-call(f32[64,64]{1,0:T(8,128)S(1)} %fusion.30), custom_call_target="Cholesky" | custom-call | tf_op jit(solution)/shard_map/jit(cholesky)/cholesky | solution.py:20
  399.4 0.6 compare_reduce_fusion
  400.0 2.1 fusion.34
  402.1 0.7 select_bitcast_fusion
  402.8 4.9 %custom-call.7 = f32[1,64,64]{1,2,0:T(8,128)S(1)} custom-call(f32[1,64,64]{2,1,0:T(8,128)S(1)} %select_bitcast_fusion), custom_call_target="InvertDiagBlocksLowerTriangular" | custom-call | tf_op jit(solution)/shard_map/jit(_solve_triangular)/triangular_solve | solution.py:22
  408.0 0.5 fusion.59
  408.5 4.0 all_to_all.19
  412.5 0.8 copy.18
  413.3 2.0 fusion.19
  415.3 0.7 dynamic-slice_add_fusion
  (25 shorter events, 2.4 us)
Async XLA Ops:
  7.2 172.0 %all-reduce.7.cloned.1.call-start = ((), (), s32[]{:S(2)}) async-start(), calls=%async_computation.1 | async-start | bytes 786432 | tf_op jit(solution)/shard_map/psum | solution.py:49
  142.2 62.6 %all-reduce.9.cloned.1.call-start = ((), (), s32[]{:S(2)}) async-start(), calls=%async_computation.2 | async-start | bytes 524288 | tf_op jit(solution)/shard_map/psum | solution.py:54
  186.8 65.1 %all-reduce.11.cloned.1.call-start = ((), (), s32[]{:S(2)}) async-start(), calls=%async_computation.3 | async-start | bytes 524288 | tf_op jit(solution)/shard_map/psum | solution.py:54
  204.8 114.3 %all-reduce.13.cloned.1.call-start = ((), (), s32[]{:S(2)}) async-start(), calls=%async_computation.4 | async-start | bytes 524288 | tf_op jit(solution)/shard_map/psum | solution.py:54
  251.9 67.3 %copy-start = (f32[1024,64]{0,1:T(8,128)S(1)}, f32[1024,64]{0,1:T(8,128)}, u32[]{:S(2)}) copy-start(f32[1024,64]{0,1:T(8,128)} %all-reduce.11.cloned.1.call-done) | copy-start | bytes 786436
  300.7 65.3 %all-reduce.15.cloned.1.call-start = ((), (), s32[]{:S(2)}) async-start(), calls=%async_computation.5 | async-start | bytes 524288 | tf_op jit(solution)/shard_map/psum | solution.py:54
Sparse Core Ops, SparseCore 0:
  142.3 36.8 all-reduce.6
  186.9 17.8 all-reduce.8
  207.7 44.1 all-reduce.10
  300.9 18.2 all-reduce.12
  321.9 44.1 all-reduce.14
